TPU v7x, 512 devices: a whole 4x8x8 slice. The times are simulated.
512 devices in a mesh: dom: 64 (over z, x, core), col: 8 (over y).
Axes of the slice: x: 4, y: 8, z: 8, core: 2. Of those that a mesh axis runs over, the one named last changes fastest.
Arguments:
- feature: bfloat16 [32768, 1024], P('dom', 'col'), may hold values from -6 to 6
- cotangent: bfloat16 [32768, 1024], P('dom', 'col'), may hold values from -6 to 6
- node_type: int32 [32768], P('dom'), may hold values from 0 to 2
- self_gain: float32 [3, 1024], P(None, 'col'), may hold values from 0.1 to 1.9
- weights: bfloat16 [8, 1024, 1024], P(None, 'dom', 'col'), may hold values from -0.1875 to 0.1875
- tile_values: bfloat16 [2048, 128, 128], P('dom'), may hold values from -0.5 to 0.5
- tile_rel: int32 [2048], P('dom'), may hold values from 0 to 7
- tile_src: int32 [2048], P('dom'), may hold values from 0 to 3
- tile_peer: int32 [2048], P('dom'), may hold values from 0 to 63, as said below
- tile_count: int32 [64], P('dom'), may hold values from 24 to 32, as said below
- send_block: int32 [64, 64], P('dom'), may hold values from -1 to 3, as said below
Outputs:
- feature_grad: bfloat16 [32768, 1024], P('dom', 'col')
- weight_grad: bfloat16 [8, 1024, 1024], P(None, None, 'col')
Inputs may be any that keep to these rules, and one draw needn't show every extreme that they name: Slots 0 to tile_count - 1 of each partition hold its tiles, the others hold none; some partition uses all 32 slots in every draw. `tile_peer`: the used slots of one partition name distinct owner partitions. send_block[o, p] is at least 0 exactly when some used slot of partition p names o, and then it is that slot's destination block within o.
All inputs are finite; a program needn't handle non-finite values.
Results may differ from a plain program's by a relative error of at most 0.0052.
Values may be sent and summed in bfloat16 or wider, within the bound.
No kernel may reach another device: no remote copies, remote signals or barrier semaphores. Data moves between devices by JAX's collectives and lax.ppermute only.
A program may use at most 64 MiB of HBM per device.

v0:
```python
import math
import jax
import jax.numpy as jnp
from jax import lax
from jax.sharding import PartitionSpec as P


def body(
    feature,
    cotangent,
    node_type,
    self_gain,
    weights,
    tile_values,
    tile_rel,
    tile_src,
    tile_peer,
    tile_count,
    send_block,
):
    partitions = lax.axis_size("dom")
    row_count, col_width = cotangent.shape
    tile_size = tile_values.shape[1]
    block_count = row_count // tile_size
    relations = weights.shape[0]
    slot_count = tile_values.shape[0]
    type_count = self_gain.shape[0]
    grad_blocks = cotangent.reshape(block_count, tile_size, col_width)
    wanted = send_block[0]
    chooser = (wanted[:, None] == jnp.arange(block_count, dtype=jnp.int32)[None, :]).astype(
        jnp.bfloat16
    )
    outgoing = jnp.einsum(
        "pb,btk->ptk", chooser, grad_blocks, preferred_element_type=jnp.float32
    ).astype(jnp.bfloat16)
    incoming = lax.all_to_all(outgoing, "dom", split_axis=0, concat_axis=0, tiled=True)
    picked = jnp.take(incoming, tile_peer, axis=0)
    contribs = jnp.einsum("tds,tdk->tsk", tile_values, picked, preferred_element_type=jnp.float32)
    is_used = jnp.arange(slot_count, dtype=jnp.int32) < tile_count[0]
    slot_of = tile_rel * block_count + tile_src
    slot_table = (
        (slot_of[None, :] == jnp.arange(relations * block_count, dtype=jnp.int32)[:, None])
        & is_used[None, :]
    ).astype(jnp.float32)
    merged = jnp.einsum("mt,tsk->msk", slot_table, contribs, precision=lax.Precision.HIGHEST)
    block_grad = merged.astype(jnp.bfloat16).reshape(relations, row_count, col_width)
    kind_table = (node_type[:, None] == jnp.arange(type_count, dtype=jnp.int32)[None, :]).astype(
        jnp.float32
    )
    self_gains = jnp.dot(kind_table, self_gain, precision=lax.Precision.HIGHEST)
    self_term = cotangent.astype(jnp.float32) * self_gains
    weight_full = lax.all_gather(weights, "dom", axis=1, tiled=True)
    weight_cols = lax.all_to_all(weight_full, "col", split_axis=1, concat_axis=2, tiled=True)
    aggregated = jnp.einsum(
        "rnk,rjk->nj",
        lax.all_gather(block_grad, "col", axis=2, tiled=True),
        weight_cols,
        preferred_element_type=jnp.float32,
    )
    feature_grad = (aggregated + self_term).astype(jnp.bfloat16)
    weight_terms = jnp.einsum(
        "nj,rnk->rjk",
        lax.all_gather(feature, "col", axis=1, tiled=True),
        block_grad,
        preferred_element_type=jnp.float32,
    )
    norm_scale = 1.0 / math.sqrt(row_count * partitions)
    summed = lax.psum(weight_terms, "dom")
    weight_grad = (summed * norm_scale).astype(jnp.bfloat16)
    return (feature_grad, weight_grad)


def solution(mesh):
    return jax.shard_map(
        body,
        mesh=mesh,
        in_specs=(
            P("dom", "col"),
            P("dom", "col"),
            P("dom"),
            P(None, "col"),
            P(None, "dom", "col"),
            P("dom", None, None),
            P("dom"),
            P("dom"),
            P("dom"),
            P("dom"),
            P("dom", None),
        ),
        out_specs=(P("dom", "col"), P(None, None, "col")),
        check_vma=False,
    )
```

profile of v0, /device:TPU:2, one launch (start us, length us, event | category | flops | bytes accessed | tf_op | source)
XLA Modules:
  0.0 470.0 jit_solution(14236573666321858946)
XLA Ops:
  7.2 0.0 copy-start
  7.2 0.0 all-gather.8.cloned.1.call-start
  7.2 0.7 all-gather.8.cloned.1.call-update
  7.9 1.7 convolution_convert_fusion
  9.6 2.7 copy.38
  12.3 0.0 copy-start.3
  12.3 0.0 copy-start.6
  12.3 0.0 copy-start.7
  12.3 0.0 copy-start.8
  12.3 14.0 %all-to-all-start = ((bf16[64,128,128]{2,1,0:T(8,128)(2,1)}), bf16[64,128,128]{2,1,0:T(8,128)(2,1)S(1)}, u32[]{:S(2)}, u32[]{:S(2)}) async-start(bf16[64,128,128]{2,1,0:T(8,128)(2,1)} %copy.38), calls=%async_computation | async-start | bytes 4194304 | tf_op jit(solution)/shard_map/all_to_all | solution.py:36
  26.3 0.0 all-gather.6.cloned.1.call-start
  26.4 0.0 copy-done.3
  26.4 0.6 copy.42
  27.0 0.1 all-gather.6.cloned.1.call-update
  27.1 0.0 all-reduce.2.cloned.1.call-start
  27.8 0.0 copy-done.6
  27.8 0.0 copy-done.7
  27.8 0.0 copy-done.8
  27.8 49.7 %all-to-all-done = bf16[64,128,128]{2,1,0:T(8,128)(2,1)S(1)} async-done(((bf16[64,128,128]{2,1,0:T(8,128)(2,1)}), bf16[64,128,128]{2,1,0:T(8,128)(2,1)S(1)}, u32[]{:S(2)}, u32[]{:S(2)}) %all-to-all-start) | async-done | bytes 2097184 | tf_op jit(solution)/shard_map/all_to_all | solution.py:36
  77.6 1.7 gather_fusion
  79.2 0.0 copy-done
  79.3 3.1 convolution_bitcast_fusion.1
  82.4 2.4 copy.40
  84.8 1.1 convolution_convert_fusion.1
  85.9 0.4 copy.41
  86.3 0.0 copy-start.1
  86.3 0.0 all-gather.8.cloned.1.call-done
  86.4 4.8 %convolution_bitcast_fusion = f32[8,1024,128]{1,2,0:T(8,128)} fusion(bf16[8,512,128]{2,1,0:T(8,128)(2,1)S(1)} %bitcast.32, bf16[512,1024]{1,0:T(8,128)(2,1)} %all-gather.8.cloned.1.call-done), kind=kOutput, calls=%fused_computation.2 | convolution fusion | flops 1073741824 | bytes 6291456 | tf_op jit(solution)/shard_map/nj,rnk->rjk/dot_general | solution.py:61
  91.2 0.0 copy-done.1
  91.2 0.0 all-reduce.2.cloned.1.call-update
  91.2 0.0 all-gather.4.cloned.1.call-start
  91.3 0.5 all-gather.4.cloned.1.call-update
  91.8 50.8 %all-gather.6.cloned.1.call-done = bf16[8,1024,128]{2,0,1:T(8,128)(2,1)} async-done(((bf16[8,16,128]{2,0,1:T(8,128)(2,1)}), bf16[8,1024,128]{2,0,1:T(8,128)(2,1)}) %all-gather.6.cloned.1.call-update) | async-done | bytes 2097168 | tf_op jit(solution)/shard_map/all_gather | solution.py:52
  142.7 6.7 %all-to-all-start.1 = ((bf16[8,1024,128]{2,0,1:T(8,128)(2,1)}), bf16[8,1024,128]{2,0,1:T(8,128)(2,1)}, u32[]{:S(2)}, u32[]{:S(2)}) async-start(bf16[8,1024,128]{2,0,1:T(8,128)(2,1)} %all-gather.6.cloned.1.call-done), calls=%async_computation.1 | async-start | bytes 4194304 | tf_op jit(solution)/shard_map/all_to_all | solution.py:53
  149.4 202.8 %all-reduce.2.cloned.1.call-done = f32[8,1024,128]{1,2,0:T(8,128)} async-done(((f32[8,1024,128]{1,2,0:T(8,128)}), f32[8,1024,128]{1,2,0:T(8,128)}) %all-reduce.2.cloned.1.call-update) | async-done | bytes 4194320 | tf_op jit(solution)/shard_map/psum | solution.py:68
  352.2 2.8 multiply_convert_fusion
  355.0 2.4 copy.45
  357.4 0.0 all-to-all-done.1
  357.4 2.9 copy.51
  360.3 2.4 all_to_all.20
  362.7 0.0 copy-start.2
  362.7 0.0 copy-start.4
  362.7 0.0 copy-start.5
  362.7 93.4 %all-gather.4.cloned.1.call-done = bf16[8,512,1024]{2,1,0:T(8,128)(2,1)} async-done(((bf16[8,512,128]{2,1,0:T(8,128)(2,1)}), bf16[8,512,1024]{2,1,0:T(8,128)(2,1)}) %all-gather.4.cloned.1.call-update) | async-done | bytes 8388624 | tf_op jit(solution)/shard_map/all_gather | solution.py:56
  456.2 6.3 %convolution_bitcast_fusion.2 = f32[512,128]{1,0:T(8,128)S(1)} fusion(bf16[8,512,1024]{2,1,0:T(8,128)(2,1)} %all-gather.4.cloned.1.call-done, bf16[8,128,1024]{2,1,0:T(8,128)(2,1)} %all_to_all.20), kind=kOutput, calls=%fused_computation.9 | convolution fusion | flops 1073741824 | bytes 10747904 | tf_op jit(solution)/shard_map/rnk,rjk->nj/dot_general | solution.py:54
  462.5 0.0 copy-done.2
  462.5 0.0 copy-done.4
  462.5 0.0 copy-done.5
  462.5 1.0 fusion.1
  (5 shorter events, 0.0 us)
Async XLA Ops:
  7.2 72.1 %copy-start = (bf16[32,128,128]{2,1,0:T(8,128)(2,1)S(1)}, bf16[32,128,128]{2,1,0:T(8,128)(2,1)}, u32[]{:S(2)}) copy-start(bf16[32,128,128]{2,1,0:T(8,128)(2,1)} %param.16) | copy-start | bytes 3145732
  7.2 79.2 %all-gather.8.cloned.1.call-start = ((), (), s32[]{:S(2)}) async-start(), calls=%async_computation.4 | async-start | bytes 1179648 | tf_op jit(solution)/shard_map/all_gather | solution.py:63
  12.3 14.1 %copy-start.3 = (bf16[8,16,128]{2,1,0:T(8,128)(2,1)S(1)}, bf16[8,16,128]{2,1,0:T(8,128)(2,1)}, u32[]{:S(2)}) copy-start(bf16[8,16,128]{2,1,0:T(8,128)(2,1)} %param.15) | copy-start | bytes 98308
  12.3 15.5 %copy-start.6 = (s32[32]{0:T(128)S(1)}, s32[32]{0:T(128)}, u32[]{:S(2)}) copy-start(s32[32]{0:T(128)} %param.19) | copy-start | bytes 388
  12.3 15.5 %copy-start.7 = (s32[32]{0:T(128)S(1)}, s32[32]{0:T(128)}, u32[]{:S(2)}) copy-start(s32[32]{0:T(128)} %param.18) | copy-start | bytes 388
  12.3 15.5 %copy-start.8 = (s32[32]{0:T(128)S(1)}, s32[32]{0:T(128)}, u32[]{:S(2)}) copy-start(s32[32]{0:T(128)} %param.17) | copy-start | bytes 388
  12.3 65.3 %all-to-all-start = ((bf16[64,128,128]{2,1,0:T(8,128)(2,1)}), bf16[64,128,128]{2,1,0:T(8,128)(2,1)S(1)}, u32[]{:S(2)}, u32[]{:S(2)}) async-start(bf16[64,128,128]{2,1,0:T(8,128)(2,1)} %copy.38), calls=%async_computation | async-start | bytes 4194304 | tf_op jit(solution)/shard_map/all_to_all | solution.py:36
  26.3 116.4 %all-gather.6.cloned.1.call-start = ((), (), s32[]{:S(2)}) async-start(), calls=%async_computation.3 | async-start | bytes 2129920 | tf_op jit(solution)/shard_map/all_gather | solution.py:52
  27.1 325.2 %all-reduce.2.cloned.1.call-start = ((), (), s32[]{:S(2)}) async-start(), calls=%async_computation.5 | async-start | bytes 8388608 | tf_op jit(solution)/shard_map/psum | solution.py:68
  86.3 4.9 %copy-start.1 = (bf16[32,128,128]{2,1,0:T(8,128)(2,1)}, bf16[32,128,128]{2,1,0:T(8,128)(2,1)S(1)}, u32[]{:S(2)}) copy-start(bf16[32,128,128]{2,1,0:T(8,128)(2,1)S(1)} %copy.41) | copy-start | bytes 3145732
  91.2 364.9 %all-gather.4.cloned.1.call-start = ((), (), s32[]{:S(2)}) async-start(), calls=%async_computation.2 | async-start | bytes 9437184 | tf_op jit(solution)/shard_map/all_gather | solution.py:56
  142.7 214.7 %all-to-all-start.1 = ((bf16[8,1024,128]{2,0,1:T(8,128)(2,1)}), bf16[8,1024,128]{2,0,1:T(8,128)(2,1)}, u32[]{:S(2)}, u32[]{:S(2)}) async-start(bf16[8,1024,128]{2,0,1:T(8,128)(2,1)} %all-gather.6.cloned.1.call-done), calls=%async_computation.1 | async-start | bytes 4194304 | tf_op jit(solution)/shard_map/all_to_all | solution.py:53
  362.7 99.8 %copy-start.2 = (bf16[512,128]{1,0:T(8,128)(2,1)S(1)}, bf16[512,128]{1,0:T(8,128)(2,1)}, u32[]{:S(2)}) copy-start(bf16[512,128]{1,0:T(8,128)(2,1)} %param.12) | copy-start | bytes 393220
  362.7 99.8 %copy-start.4 = (f32[3,128]{1,0:T(4,128)S(1)}, f32[3,128]{1,0:T(4,128)}, u32[]{:S(2)}) copy-start(f32[3,128]{1,0:T(4,128)} %param.14) | copy-start | bytes 4612
  362.7 99.8 %copy-start.5 = (s32[512]{0:T(512)S(1)}, s32[512]{0:T(512)}, u32[]{:S(2)}) copy-start(s32[512]{0:T(512)} %param.13) | copy-start | bytes 6148
Sparse Core Ops, SparseCore 0:
  10.0 46.7 all-gather.7
  60.7 81.9 all-gather.5
  146.2 205.9 all-reduce.1
  354.3 101.8 all-gather.3
where the time goes:
time: 471 us; the launch traced here: 470 us
  waiting for transfers between devices  398 us (85%)
  starting transfers between devices  20.9 us (4%)
  matrix products  18.1 us (4%)
  local copies, waits for them, and re-layouts  15.5 us (3%)
  between operations  14.6 us (3%)
    psum x1, waiting for transfers between devices, body(): summed = lax.psum(weight_terms, 'dom')  203 us
    all_gather x1, waiting for transfers between devices, body(): lax.all_gather(block_grad, 'col', axis=2, tiled=True)  93.4 us
    all_gather x1, waiting for transfers between devices, body(): weight_full = lax.all_gather(weights, 'dom', axis=1, tiled=True)  50.8 us
    all_to_all x1, waiting for transfers between devices, body(): lax.all_to_all(outgoing, 'dom', split_axis=0, concat_axis=0, tiled=True)  49.7 us
    all_to_all x1, starting transfers between devices, body(): lax.all_to_all(outgoing, 'dom', split_axis=0, concat_axis=0, tiled=True)  14 us
  transfers between devices with their start and end apart: 6, of which 4 were waited for; matrix products, arithmetic and copies ran while one was open for 6% of the time, Pallas kernels for 0%

commit v1 on v0

--- a/solution.py
+++ b/solution.py
@@ -3,6 +3,19 @@
 import jax.numpy as jnp
 from jax import lax
 from jax.sharding import PartitionSpec as P
+
+
+def collect(value, axis, dim):
+    ways = lax.axis_size(axis)
+    up = [(d, (d + 1) % ways) for d in range(ways)]
+    down = [(d, (d - 1) % ways) for d in range(ways)]
+    earlier, later = ([value], [value])
+    for _ in range(ways // 2):
+        earlier.append(lax.ppermute(earlier[-1], axis, up))
+    for _ in range((ways - 1) // 2):
+        later.append(lax.ppermute(later[-1], axis, down))
+    line = jnp.concatenate([*earlier[::-1], *later[1:]], axis=dim)
+    return jnp.roll(line, (lax.axis_index(axis) - ways // 2) * value.shape[dim], axis=dim)
 
 
 def body(
@@ -53,7 +66,7 @@
     weight_cols = lax.all_to_all(weight_full, "col", split_axis=1, concat_axis=2, tiled=True)
     aggregated = jnp.einsum(
         "rnk,rjk->nj",
-        lax.all_gather(block_grad, "col", axis=2, tiled=True),
+        collect(block_grad, "col", 2),
         weight_cols,
         preferred_element_type=jnp.float32,
     )

time: 471 us -> 441 us (0.936)
  the two profiles are of different devices: /device:TPU:2 before, /device:TPU:8 now
where the time goes in v1:
time: 441 us; the launch traced here: 439 us
  waiting for transfers between devices  316 us (72%)
  starting transfers between devices  45.2 us (10%)
  local copies, waits for them, and re-layouts  43 us (10%)
  between operations  14.7 us (3%)
  matrix products  14.2 us (3%)
  other arithmetic  6.14 us (1%)
    psum x1, waiting for transfers between devices, body(): summed = lax.psum(weight_terms, 'dom')  167 us
    all_to_all x1, waiting for transfers between devices, body(): lax.all_to_all(outgoing, 'dom', split_axis=0, concat_axis=0, tiled=True)  49 us
    all_gather x1, waiting for transfers between devices, body(): lax.all_gather(feature, 'col', axis=1, tiled=True)  46 us
    ppermute x4, waiting for transfers between devices, collect(): earlier.append(lax.ppermute(earlier[-1], axis, up))  43.3 us
    unnamed x27, local copies, waits for them, and re-layouts  24.5 us
    ppermute x4, starting transfers between devices, collect(): earlier.append(lax.ppermute(earlier[-1], axis, up))  14.9 us
    all_to_all x1, starting transfers between devices, body(): lax.all_to_all(outgoing, 'dom', split_axis=0, concat_axis=0, tiled=True)  14.2 us
    all_gather x1, waiting for transfers between devices, body(): weight_full = lax.all_gather(weights, 'dom', axis=1, tiled=True)  10.3 us
  transfers between devices with their start and end apart: 12, of which 7 were waited for; matrix products, arithmetic and copies ran while one was open for 10% of the time, Pallas kernels for 0%

profile of v1, /device:TPU:8, one launch (start us, length us, event | category | flops | bytes accessed | tf_op | source)
XLA Modules:
  0.0 439.4 jit_solution(6450090993352072609)
XLA Ops:
  7.2 0.0 copy-start
  7.2 0.0 all-gather.3.cloned.1.call-start
  7.2 1.5 copy.42
  8.7 0.0 all-gather.3.cloned.1.call-update
  8.7 1.7 convolution_convert_fusion
  10.4 2.7 copy.38
  13.1 14.2 %all-to-all-start = ((bf16[64,128,128]{2,1,0:T(8,128)(2,1)}), bf16[64,128,128]{2,1,0:T(8,128)(2,1)}, u32[]{:S(2)}, u32[]{:S(2)}) async-start(bf16[64,128,128]{2,1,0:T(8,128)(2,1)} %copy.38), calls=%async_computation | async-start | bytes 4194304 | tf_op jit(solution)/shard_map/all_to_all | solution.py:49
  27.3 0.0 all-gather.5.cloned.1.call-start
  27.3 0.7 all-gather.5.cloned.1.call-update
  28.7 0.7 compare_select_fusion
  29.4 0.7 compare_and_fusion
  30.0 0.7 multiply_add_fusion
  30.7 49.0 %all-to-all-done = bf16[64,128,128]{2,1,0:T(8,128)(2,1)} async-done(((bf16[64,128,128]{2,1,0:T(8,128)(2,1)}), bf16[64,128,128]{2,1,0:T(8,128)(2,1)}, u32[]{:S(2)}, u32[]{:S(2)}) %all-to-all-start) | async-done | bytes 2097184 | tf_op jit(solution)/shard_map/all_to_all | solution.py:49
  79.7 2.4 gather_fusion
  82.1 0.0 copy-done
  82.1 1.9 convolution_bitcast_fusion.1
  84.0 3.1 copy.40
  87.1 2.7 convolution_convert_fusion.1
  89.8 0.4 copy.41
  90.2 3.5 collective-permute-start
  93.8 10.3 %all-gather.3.cloned.1.call-done = bf16[8,1024,128]{2,0,1:T(8,128)(2,1)} async-done(((bf16[8,16,128]{2,0,1:T(8,128)(2,1)}), bf16[8,1024,128]{2,0,1:T(8,128)(2,1)}) %all-gather.3.cloned.1.call-update) | async-done | bytes 2097168 | tf_op jit(solution)/shard_map/all_gather | solution.py:65
  104.1 7.3 %all-to-all-start.1 = ((bf16[8,1024,128]{2,0,1:T(8,128)(2,1)}), bf16[8,1024,128]{2,0,1:T(8,128)(2,1)}, u32[]{:S(2)}, u32[]{:S(2)}) async-start(bf16[8,1024,128]{2,0,1:T(8,128)(2,1)} %all-gather.3.cloned.1.call-done), calls=%async_computation.1 | async-start | bytes 4194304 | tf_op jit(solution)/shard_map/all_to_all | solution.py:66
  111.4 0.0 all-reduce.2.cloned.1.call-start
  111.4 15.6 %collective-permute-done = bf16[8,512,128]{2,1,0:T(8,128)(2,1)S(1)} collective-permute-done((bf16[8,512,128]{2,1,0:T(8,128)(2,1)S(1)}, bf16[8,512,128]{2,1,0:T(8,128)(2,1)S(1)}, u32[]{:S(2)}, u32[]{:S(2)}) %collective-permute-start) | collective-permute-done | bytes 1048608 | tf_op jit(solution)/shard_map/ppermute | solution.py:14
  127.0 5.3 %collective-permute-start.1 = (bf16[8,512,128]{2,1,0:T(8,128)(2,1)S(1)}, bf16[8,512,128]{2,1,0:T(8,128)(2,1)}, u32[]{:S(2)}, u32[]{:S(2)}) collective-permute-start(bf16[8,512,128]{2,1,0:T(8,128)(2,1)S(1)} %collective-permute-done), channel_id=1, source_target_pairs={{0,1},{1,2},{2,3},{3,4},{4,5},{5,6},{6,7},{7,0},{8,9},{9,10},{10,1... | collective-permute-start | bytes 3145736 | tf_op jit(solution)/shard_map/ppermute | solution.py:14
  132.2 1.9 collective-permute-start.4
  134.2 46.0 %all-gather.5.cloned.1.call-done = bf16[512,1024]{1,0:T(8,128)(2,1)} async-done(((bf16[512,128]{1,0:T(8,128)(2,1)}), bf16[512,1024]{1,0:T(8,128)(2,1)}) %all-gather.5.cloned.1.call-update) | async-done | bytes 1048592 | tf_op jit(solution)/shard_map/all_gather | solution.py:76
  180.1 4.5 %convolution_bitcast_fusion = f32[8,1024,128]{1,2,0:T(8,128)} fusion(bf16[8,512,128]{2,1,0:T(8,128)(2,1)S(1)} %bitcast.41, bf16[512,1024]{1,0:T(8,128)(2,1)} %all-gather.5.cloned.1.call-done), kind=kOutput, calls=%fused_computation.4 | convolution fusion | flops 1073741824 | bytes 6291456 | tf_op jit(solution)/shard_map/nj,rnk->rjk/dot_general | solution.py:74
  184.6 0.0 all-reduce.2.cloned.1.call-update
  184.7 8.2 %collective-permute-done.1 = bf16[8,512,128]{2,1,0:T(8,128)(2,1)} collective-permute-done((bf16[8,512,128]{2,1,0:T(8,128)(2,1)S(1)}, bf16[8,512,128]{2,1,0:T(8,128)(2,1)}, u32[]{:S(2)}, u32[]{:S(2)}) %collective-permute-start.1) | collective-permute-done | bytes 1048608 | tf_op jit(solution)/shard_map/ppermute | solution.py:14
  192.9 3.5 collective-permute-start.2
  196.4 0.0 collective-permute-done.4
  196.4 2.6 collective-permute-start.5
  199.0 19.5 %collective-permute-done.2 = bf16[8,512,128]{2,1,0:T(8,128)(2,1)} collective-permute-done((bf16[8,512,128]{2,1,0:T(8,128)(2,1)}, bf16[8,512,128]{2,1,0:T(8,128)(2,1)}, u32[]{:S(2)}, u32[]{:S(2)}) %collective-permute-start.2) | collective-permute-done | bytes 1048608 | tf_op jit(solution)/shard_map/ppermute | solution.py:14
  218.4 2.6 collective-permute-start.3
  221.1 0.0 copy-done.2
  221.1 0.3 convolution_multiply_fusion
  221.4 0.0 collective-permute-done.5
  221.5 4.3 collective-permute-start.6
  225.8 166.7 %all-reduce.2.cloned.1.call-done = f32[8,1024,128]{1,2,0:T(8,128)} async-done(((f32[8,1024,128]{1,2,0:T(8,128)}), f32[8,1024,128]{1,2,0:T(8,128)}) %all-reduce.2.cloned.1.call-update) | async-done | bytes 4194320 | tf_op jit(solution)/shard_map/psum | solution.py:81
  392.5 4.1 multiply_convert_fusion
  396.6 3.9 copy.45
  400.5 0.0 all-to-all-done.1
  400.5 4.2 copy.51
  404.8 4.2 all_to_all.20
  408.9 0.0 collective-permute-done.3
  408.9 1.7 constant_dynamic-update-slice_fusion.15
  410.6 1.6 constant_dynamic-update-slice_fusion.14
  412.2 1.6 constant_dynamic-update-slice_fusion.13
  413.8 0.4 constant_dynamic-update-slice_fusion.12
  414.2 0.4 constant_dynamic-update-slice_fusion.11
  414.6 1.6 constant_dynamic-update-slice_fusion.10
  416.2 1.6 constant_dynamic-update-slice_fusion.9
  417.8 0.0 collective-permute-done.6
  417.8 1.6 constant_dynamic-update-slice_fusion.8
  419.4 1.6 constant_dynamic-update-slice_fusion.7
  421.0 1.6 constant_dynamic-update-slice_fusion.6
  422.6 1.6 constant_dynamic-update-slice_fusion.5
  424.2 0.4 constant_dynamic-update-slice_fusion.4
  424.6 0.4 constant_dynamic-update-slice_fusion.3
  424.9 1.6 constant_dynamic-update-slice_fusion.2
  426.5 1.6 constant_dynamic-update-slice_fusion.1
  428.1 1.6 constant_dynamic-update-slice_fusion
  429.8 3.1 fusion.8
  (9 shorter events, 0.0 us)
Async XLA Ops:
  7.2 74.9 %copy-start = (bf16[32,128,128]{2,1,0:T(8,128)(2,1)S(1)}, bf16[32,128,128]{2,1,0:T(8,128)(2,1)}, u32[]{:S(2)}) copy-start(bf16[32,128,128]{2,1,0:T(8,128)(2,1)} %param.16) | copy-start | bytes 3145732
  7.2 96.9 %all-gather.3.cloned.1.call-start = ((), (), s32[]{:S(2)}) async-start(), calls=%async_computation.2 | async-start | bytes 2129920 | tf_op jit(solution)/shard_map/all_gather | solution.py:65
  13.1 208.0 %copy-start.2 = (bf16[512,128]{1,0:T(8,128)(2,1)S(1)}, bf16[512,128]{1,0:T(8,128)(2,1)}, u32[]{:S(2)}) copy-start(bf16[512,128]{1,0:T(8,128)(2,1)} %param.12) | copy-start | bytes 393220
  13.1 208.0 %copy-start.3 = (f32[3,128]{1,0:T(4,128)S(1)}, f32[3,128]{1,0:T(4,128)}, u32[]{:S(2)}) copy-start(f32[3,128]{1,0:T(4,128)} %param.14) | copy-start | bytes 4612
  13.1 208.0 %copy-start.4 = (s32[512]{0:T(512)S(1)}, s32[512]{0:T(512)}, u32[]{:S(2)}) copy-start(s32[512]{0:T(512)} %param.13) | copy-start | bytes 6148
  13.1 66.6 %all-to-all-start = ((bf16[64,128,128]{2,1,0:T(8,128)(2,1)}), bf16[64,128,128]{2,1,0:T(8,128)(2,1)}, u32[]{:S(2)}, u32[]{:S(2)}) async-start(bf16[64,128,128]{2,1,0:T(8,128)(2,1)} %copy.38), calls=%async_computation | async-start | bytes 4194304 | tf_op jit(solution)/shard_map/all_to_all | solution.py:49
  27.3 152.9 %all-gather.5.cloned.1.call-start = ((), (), s32[]{:S(2)}) async-start(), calls=%async_computation.3 | async-start | bytes 1179648 | tf_op jit(solution)/shard_map/all_gather | solution.py:76
  90.2 36.7 %collective-permute-start = (bf16[8,512,128]{2,1,0:T(8,128)(2,1)S(1)}, bf16[8,512,128]{2,1,0:T(8,128)(2,1)S(1)}, u32[]{:S(2)}, u32[]{:S(2)}) collective-permute-start(bf16[8,512,128]{2,1,0:T(8,128)(2,1)S(1)} %bitcast.39), channel_id=1, source_target_pairs={{0,1},{1,2},{2,3},{3,4},{4,5},{5,6},{6,7},{7,0},{8,9},{9,10},{10,1... | collective-permute-start | bytes 3145736 | tf_op jit(solution)/shard_map/ppermute | solution.py:14
  104.1 296.4 %all-to-all-start.1 = ((bf16[8,1024,128]{2,0,1:T(8,128)(2,1)}), bf16[8,1024,128]{2,0,1:T(8,128)(2,1)}, u32[]{:S(2)}, u32[]{:S(2)}) async-start(bf16[8,1024,128]{2,0,1:T(8,128)(2,1)} %all-gather.3.cloned.1.call-done), calls=%async_computation.1 | async-start | bytes 4194304 | tf_op jit(solution)/shard_map/all_to_all | solution.py:66
  111.4 281.1 %all-reduce.2.cloned.1.call-start = ((), (), s32[]{:S(2)}) async-start(), calls=%async_computation.4 | async-start | bytes 8388608 | tf_op jit(solution)/shard_map/psum | solution.py:81
  127.0 65.9 %collective-permute-start.1 = (bf16[8,512,128]{2,1,0:T(8,128)(2,1)S(1)}, bf16[8,512,128]{2,1,0:T(8,128)(2,1)}, u32[]{:S(2)}, u32[]{:S(2)}) collective-permute-start(bf16[8,512,128]{2,1,0:T(8,128)(2,1)S(1)} %collective-permute-done), channel_id=1, source_target_pairs={{0,1},{1,2},{2,3},{3,4},{4,5},{5,6},{6,7},{7,0},{8,9},{9,10},{10,1... | collective-permute-start | bytes 3145736 | tf_op jit(solution)/shard_map/ppermute | solution.py:14
  132.2 64.1 %collective-permute-start.4 = (bf16[8,512,128]{2,1,0:T(8,128)(2,1)S(1)}, bf16[8,512,128]{2,1,0:T(8,128)(2,1)}, u32[]{:S(2)}, u32[]{:S(2)}) collective-permute-start(bf16[8,512,128]{2,1,0:T(8,128)(2,1)S(1)} %bitcast.40), channel_id=1, source_target_pairs={{0,7},{1,0},{2,1},{3,2},{4,3},{5,4},{6,5},{7,6},{8,15},{9,8},{10,9... | collective-permute-start | bytes 3145736 | tf_op jit(solution)/shard_map/ppermute | solution.py:16
  192.9 25.5 %collective-permute-start.2 = (bf16[8,512,128]{2,1,0:T(8,128)(2,1)}, bf16[8,512,128]{2,1,0:T(8,128)(2,1)}, u32[]{:S(2)}, u32[]{:S(2)}) collective-permute-start(bf16[8,512,128]{2,1,0:T(8,128)(2,1)} %collective-permute-done.1), channel_id=1, source_target_pairs={{0,1},{1,2},{2,3},{3,4},{4,5},{5,6},{6,7},{7,0},{8,9},{9,10},{10,1... | collective-permute-start | bytes 3145736 | tf_op jit(solution)/shard_map/ppermute | solution.py:14
  196.4 25.1 %collective-permute-start.5 = (bf16[8,512,128]{2,1,0:T(8,128)(2,1)}, bf16[8,512,128]{2,1,0:T(8,128)(2,1)}, u32[]{:S(2)}, u32[]{:S(2)}) collective-permute-start(bf16[8,512,128]{2,1,0:T(8,128)(2,1)} %collective-permute-done.4), channel_id=1, source_target_pairs={{0,7},{1,0},{2,1},{3,2},{4,3},{5,4},{6,5},{7,6},{8,15},{9,8},{10,9... | collective-permute-start | bytes 3145736 | tf_op jit(solution)/shard_map/ppermute | solution.py:16
  218.4 190.5 %collective-permute-start.3 = (bf16[8,512,128]{2,1,0:T(8,128)(2,1)}, bf16[8,512,128]{2,1,0:T(8,128)(2,1)}, u32[]{:S(2)}, u32[]{:S(2)}) collective-permute-start(bf16[8,512,128]{2,1,0:T(8,128)(2,1)} %collective-permute-done.2), channel_id=1, source_target_pairs={{0,1},{1,2},{2,3},{3,4},{4,5},{5,6},{6,7},{7,0},{8,9},{9,10},{10,1... | collective-permute-start | bytes 3145736 | tf_op jit(solution)/shard_map/ppermute | solution.py:14
  221.5 196.3 %collective-permute-start.6 = (bf16[8,512,128]{2,1,0:T(8,128)(2,1)}, bf16[8,512,128]{2,1,0:T(8,128)(2,1)}, u32[]{:S(2)}, u32[]{:S(2)}) collective-permute-start(bf16[8,512,128]{2,1,0:T(8,128)(2,1)} %collective-permute-done.5), channel_id=1, source_target_pairs={{0,7},{1,0},{2,1},{3,2},{4,3},{5,4},{6,5},{7,6},{8,15},{9,8},{10,9... | collective-permute-start | bytes 3145736 | tf_op jit(solution)/shard_map/ppermute | solution.py:16
  408.9 20.8 %copy-start.1 = (bf16[8,128,1024]{2,1,0:T(8,128)(2,1)S(1)}, bf16[8,128,1024]{2,1,0:T(8,128)(2,1)}, u32[]{:S(2)}) copy-start(bf16[8,128,1024]{2,1,0:T(8,128)(2,1)} %all_to_all.20) | copy-start | bytes 6291460
Sparse Core Ops, SparseCore 0:
  11.9 92.1 all-gather.2
  106.1 73.9 all-gather.4
  184.8 207.6 all-reduce.1
